TPU v7x, 32 devices: a whole 2x2x4 slice. The times are simulated.
32 devices in a mesh: leaf: 2 (over y), user: 4 (over x, core), tensor: 4 (over z).
Axes of the slice: x: 2, y: 2, z: 4, core: 2. Of those that a mesh axis runs over, the one named last changes fastest.
Arguments:
- user_feat: bfloat16 [32, 128], P('user'), may hold values from -6 to 6
- beam_nodes: int32 [32, 128], P('user', ('leaf', 'tensor')), may hold values from 0 to 16383, as said below
- item_ids: int32 [32, 384], P('user', 'leaf'), may hold values from 0 to 16383, as said below
- subtree_slot: int32 [32], replicated, may hold values from 0 to 31, as said below
- node_table: bfloat16 [16384, 128], P(('leaf', 'tensor')), may hold values from -6 to 6
- item_table: bfloat16 [16384, 128], P(('leaf', 'tensor')), may hold values from -6 to 6
- mlp_user: bfloat16 [128, 1024], replicated, may hold values from -0.375 to 0.375
- mlp_node: bfloat16 [128, 1024], replicated, may hold values from -0.375 to 0.375
- mlp_bias: float32 [1024], replicated, may hold values from -3 to 3
- mlp_out: bfloat16 [1024], replicated, may hold values from -0.1875 to 0.1875
- proj_in: bfloat16 [384, 2048], P(None, 'tensor'), may hold values from -0.3125 to 0.3125
- cross_w: bfloat16 [2, 2048, 2048], P(None, None, 'tensor'), may hold values from -0.125 to 0.125
- cross_b: float32 [2, 2048], P(None, 'tensor'), may hold values from -3 to 3
- out_w: bfloat16 [2048], P('tensor'), may hold values from -0.125 to 0.125
Outputs:
- beam_score: float32 [32, 128], P('user', ('leaf', 'tensor'))
- interest: float32 [32, 128], P('user')
- logit: float32 [32, 384], P('user', 'leaf')
Inputs may be any that keep to these rules, and one draw needn't show every extreme that they name: A permutation of the subtrees: subtree s is held by index subtree_slot[s] // 4 of leaf+tensor (leaf-major), as its block subtree_slot[s] % 4. `beam_nodes`: within the 8 x 16 block of one device, at most 16 nodes belong to subtrees held by any one index of leaf+tensor; some index receives exactly 16 from every device's block. `item_ids`: split a device's 8 x 192 block, flattened user by user, into 4 runs of 384 items; each run has at most 48 items of subtrees held by any one index of leaf+tensor, and some index receives exactly 48 from every run.
All inputs are finite; a program needn't handle non-finite values.
Results may differ from a plain program's by a relative error of at most 0.0062.
Values may be sent and summed in bfloat16 or wider, within the bound.
A program may use at most 64 MiB of HBM per device.

v0:
```python
import math
import jax
import jax.numpy as jnp
from jax import lax
from jax.sharding import PartitionSpec as P

SUB_NODES = 512
SUB_ITEMS = 512
BOTH = ("leaf", "tensor")
F32 = jnp.float32
BF16 = jnp.bfloat16


def small_lookup(table, index):
    hits = index[..., None] == jnp.arange(table.shape[0], dtype=jnp.int32)
    return jnp.sum(jnp.where(hits, table, 0), axis=-1)


def locate(ids, span, subtree_slot, rows):
    slot = small_lookup(subtree_slot, ids // span)
    per = rows // span
    return (slot // per, slot % per * span + ids % span)


def rank_in_row(marks):
    n = marks.shape[-1]
    at = jnp.arange(n, dtype=jnp.int32)
    before = (at[:, None] < at[None, :]).astype(BF16)
    return jnp.dot(marks.astype(BF16), before, preferred_element_type=F32).astype(jnp.int32)


def pick_rows(table, wanted):
    hot = (wanted[:, None] == jnp.arange(table.shape[0], dtype=jnp.int32)[None, :]).astype(BF16)
    return jnp.dot(hot, table, preferred_element_type=F32).astype(BF16)


def owned_slots(owner, local, me, cap):
    mine = owner == me
    rank = rank_in_row(mine)
    chosen = mine[:, None, :] & (
        rank[:, None, :] == jnp.arange(cap, dtype=jnp.int32)[None, :, None]
    )
    wanted = jnp.sum(jnp.where(chosen, local[:, None, :] + 1, 0), axis=2) - 1
    return (chosen, wanted)


def per_device(
    user_feat,
    beam_nodes,
    item_ids,
    subtree_slot,
    node_table,
    item_table,
    mlp_user,
    mlp_node,
    mlp_bias,
    mlp_out,
    proj_in,
    cross_w,
    cross_b,
    out_w,
):
    leafs = lax.axis_size("leaf")
    tensors = lax.axis_size("tensor")
    owners = leafs * tensors
    tensor_at = lax.axis_index("tensor")
    me = lax.axis_index("leaf") * tensors + tensor_at
    users, beam = beam_nodes.shape
    items = item_ids.shape[1]
    width = user_feat.shape[1]
    proj_all = lax.all_gather(proj_in, "tensor", axis=1, tiled=True)
    first_here = jnp.dot(proj_all, cross_w[0], preferred_element_type=F32).astype(BF16)
    first_all = lax.all_gather(first_here, "tensor", axis=1, tiled=True)
    bias_all = lax.all_gather(cross_b[0], "tensor", axis=0, tiled=True)
    requests = users * beam
    cap_b = max(2, -(-requests // owners))
    node_ids = lax.all_gather(beam_nodes.reshape(-1), BOTH, axis=0)
    n_owner, n_local = locate(node_ids, SUB_NODES, subtree_slot, node_table.shape[0])
    n_chosen, n_wanted = owned_slots(n_owner, n_local, me, cap_b)
    asker = jnp.arange(requests, dtype=jnp.int32) // beam
    n_user = jnp.sum(jnp.where(n_chosen, asker[None, None, :], 0), axis=2).reshape(-1)
    node_rows = pick_rows(node_table, n_wanted.reshape(-1))
    user_hot = n_user[:, None] == jnp.arange(users, dtype=jnp.int32)[None, :]
    user_rows = jnp.dot(user_hot.astype(BF16), user_feat, preferred_element_type=F32).astype(BF16)
    pre = (
        jnp.dot(user_rows, mlp_user, preferred_element_type=F32)
        + jnp.dot(node_rows, mlp_node, preferred_element_type=F32)
        + mlp_bias
    )
    hidden = jax.nn.silu(pre).astype(BF16)
    scores = jnp.dot(hidden, mlp_out, preferred_element_type=F32)
    held = n_wanted.reshape(-1) >= 0
    gate = jnp.where(user_hot & held[:, None], jax.nn.sigmoid(scores)[:, None], 0.0)
    numerator = lax.dot_general(
        gate, node_rows.astype(F32), (((0,), (0,)), ((), ())), precision=lax.Precision.HIGHEST
    )
    back = jnp.sum(jnp.where(n_chosen, scores.reshape(owners, cap_b, 1), 0.0), axis=1)
    summed = lax.psum(jnp.concatenate([numerator.reshape(-1), back.reshape(-1)]), BOTH)
    interest = summed[: users * width].reshape(users, width) / math.sqrt(owners * beam)
    beam_score = lax.dynamic_slice(summed, (users * width + me * requests,), (requests,)).reshape(
        users, beam
    )
    rows = users * items
    fetch = rows // tensors
    cap_i = max(2, -(-fetch // owners))
    item_all = lax.all_gather(item_ids.reshape(-1), "leaf", axis=0).reshape(owners, fetch)
    i_owner, i_local = locate(item_all, SUB_ITEMS, subtree_slot, item_table.shape[0])
    _, i_wanted = owned_slots(i_owner, i_local, me, cap_i)
    sent = pick_rows(item_table, i_wanted.reshape(-1)).reshape(owners, cap_i, width)
    arrived = lax.all_to_all(sent, BOTH, split_axis=0, concat_axis=0, tiled=True)
    my_owner = lax.dynamic_slice(i_owner, (me, 0), (1, fetch))[0]
    marks = my_owner[None, :] == jnp.arange(owners, dtype=jnp.int32)[:, None]
    place = jnp.sum(jnp.where(marks, rank_in_row(marks), 0), axis=0) + my_owner * cap_i
    run_rows = pick_rows(arrived.reshape(owners * cap_i, width), place)
    item_rows = lax.all_gather(run_rows, "tensor", axis=0, tiled=True)
    shared = jnp.concatenate([user_feat, interest.astype(BF16)], axis=1)
    two = 2 * width
    base0 = jnp.dot(shared, proj_all[:two], preferred_element_type=F32)
    base1 = jnp.dot(shared, first_all[:two], preferred_element_type=F32) + bias_all
    x0 = jnp.dot(item_rows, proj_all[two:], preferred_element_type=F32).reshape(users, items, -1)
    mixed = jnp.dot(item_rows, first_all[two:], preferred_element_type=F32).reshape(
        users, items, -1
    )
    x0 = x0 + base0[:, None, :]
    mixed = mixed + base1[:, None, :]
    x1 = (x0 * mixed + x0).astype(BF16).reshape(rows, -1)
    second = jnp.dot(x1, cross_w[1], preferred_element_type=F32)
    cols = proj_in.shape[1]
    x0_here = lax.dynamic_slice(
        x0.astype(BF16).reshape(rows, -1), (0, tensor_at * cols), (rows, cols)
    )
    x1_here = lax.dynamic_slice(x1, (0, tensor_at * cols), (rows, cols))
    x2 = x0_here.astype(F32) * (second + cross_b[1]) + x1_here.astype(F32)
    partial = jnp.sum(x2 * out_w.astype(F32), axis=1)
    logit = lax.psum(partial, "tensor").reshape(users, items)
    return (beam_score, interest, logit)


def solution(mesh):
    placed = (
        P("user", None),
        P("user", BOTH),
        P("user", "leaf"),
        P(),
        P(BOTH, None),
        P(BOTH, None),
        P(),
        P(),
        P(),
        P(),
        P(None, "tensor"),
        P(None, None, "tensor"),
        P(None, "tensor"),
        P("tensor"),
    )
    return jax.shard_map(
        per_device,
        mesh=mesh,
        in_specs=placed,
        out_specs=(P("user", BOTH), P("user", None), P("user", "leaf")),
        check_vma=False,
    )
```

profile of v0, /device:TPU:0, one launch (start us, length us, event | category | flops | bytes accessed | tf_op | source)
XLA Modules:
  0.0 145.1 jit_solution(10727582794574176062)
XLA Ops:
  7.2 0.7 all-gather.6.cloned.1.call-update
  7.9 0.8 reshape.212
  8.7 5.3 %all-gather.2 = s32[2,1,1536]{2,1,0:T(1,128)S(1)} all-gather(s32[1,1,1536]{2,1,0:T(1,128)S(1)} %reshape.212), channel_id=1, replica_groups=mesh['leaf'=2,'user'=4,'tensor'=4] {'leaf'}, dimensions={0}, use_global_device_ids=true | all-gather | bytes 18432 | tf_op jit(solution)/shard_map/all_gather | solution.py:106
  14.1 0.8 select_reduce_fusion.1
  15.1 0.2 select_reduce_fusion
  15.4 1.3 fusion.18
  16.8 6.4 %all-to-all-start = ((bf16[8,48,128]{2,1,0:T(8,128)(2,1)}), bf16[8,48,128]{2,1,0:T(8,128)(2,1)S(1)}, u32[]{:S(2)}, u32[]{:S(2)}) async-start(bf16[8,48,128]{2,1,0:T(8,128)(2,1)} %bitcast.5), calls=%async_computation | async-start | bytes 196608 | tf_op jit(solution)/shard_map/all_to_all | solution.py:110
  23.2 0.8 reshape.210
  23.9 0.7 convert_element_type.72
  24.6 21.6 %all-gather.1 = s32[8,1,128]{2,1,0:T(1,128)S(1)} all-gather(s32[1,1,128]{2,1,0:T(1,128)S(1)} %reshape.210), channel_id=1, replica_groups=mesh['leaf'=2,'user'=4,'tensor'=4] {'leaf','tensor'}, dimensions={0}, use_global_device_ids=true | all-gather | bytes 4608 | tf_op jit(solution)/shard_map/all_gather | solution.py:77
  46.2 0.7 select_reduce_fusion.2
  47.1 0.3 select_reduce_fusion.4
  47.7 0.7 reshape.217
  48.3 1.3 fusion.19
  49.7 1.8 %all-gather.6.cloned.1.call-done = bf16[384,2048]{1,0:T(8,128)(2,1)} async-done(((bf16[384,512]{1,0:T(8,128)(2,1)}), bf16[384,2048]{1,0:T(8,128)(2,1)}) %all-gather.6.cloned.1.call-update) | async-done | bytes 1572880 | tf_op jit(solution)/shard_map/all_gather | solution.py:71
  51.5 3.8 %fusion.14 = bf16[384,512]{1,0:T(8,128)(2,1)} fusion(bf16[384,2048]{1,0:T(8,128)(2,1)} %all-gather.6.cloned.1.call-done, bf16[2,2048,512]{2,1,0:T(8,128)(2,1)} %param.25), kind=kOutput, calls=%fused_computation.19 | convolution fusion | flops 805502976 | bytes 4063232 | tf_op jit(solution)/shard_map/dot_general | solution.py:72
  55.4 1.0 convolution_convert_fusion.1
  56.3 1.2 add_divide_fusion
  57.7 1.1 convolution_bitcast_fusion
  58.8 21.1 %psum.14 = f32[2048]{0:T(1024)S(1)} all-reduce(f32[2048]{0:T(1024)S(1)} %pad_maximum_fusion), channel_id=1, replica_groups=mesh['leaf'=2,'user'=4,'tensor'=4] {'leaf','tensor'}, use_global_device_ids=true, to_apply=%region_4.5 | all-reduce | flops 2048 | bytes 16384 | tf_op jit(solution)/shard_map/psum | solution.py:98
  80.0 0.7 reshape.204
  80.7 12.6 %all-gather = f32[1,2048]{1,0:T(1,128)S(1)} all-gather(f32[1,512]{1,0:T(1,128)S(1)} %get-tuple-element.10), channel_id=2, replica_groups=mesh['leaf'=2,'user'=4,'tensor'=4] {'tensor'}, dimensions={1}, use_global_device_ids=true | all-gather | bytes 10240 | tf_op jit(solution)/shard_map/all_gather | solution.py:74
  93.3 0.2 fusion.21
  93.5 0.6 fusion.63
  94.1 0.3 convolution_convert_fusion
  94.4 14.2 %all_gather.20 = bf16[1536,128]{1,0:T(8,128)(2,1)S(1)} all-gather(bf16[384,128]{1,0:T(8,128)(2,1)S(1)} %convolution_convert_fusion), channel_id=1, replica_groups=mesh['leaf'=2,'user'=4,'tensor'=4] {'tensor'}, dimensions={0}, use_global_device_ids=true | all-gather | bytes 491520 | tf_op jit(solution)/shard_map/all_gather | solution.py:115
  108.6 0.2 fusion.23
  108.8 6.4 %bitcast_add_fusion.1 = f32[1536,2048]{1,0:T(8,128)} fusion(bf16[1536,128]{1,0:T(8,128)(2,1)S(1)} %all_gather.20, f32[8,2048]{1,0:T(8,128)S(1)} %fusion.23, bf16[384,2048]{1,0:T(8,128)(2,1)S(1)} %copy-done.1), kind=kOutput, calls=%fused_computation.3 | convolution fusion | flops 808452096 | bytes 13565952 | tf_op jit(solution)/shard_map/dot_general | solution.py:120
  115.2 1.5 %convolution_add_fusion.1 = f32[8,2048]{1,0:T(8,128)S(1)} fusion(bf16[384,2048]{1,0:T(8,128)(2,1)} %all-gather.8.cloned.1.call-done, f32[2048]{0:T(1024)S(1)} %bitcast.47, bf16[8,128]{1,0:T(8,128)(2,1)S(1)} %get-tuple-element.5, bf16[8,128]{1,0:T(8,128)(2,1)S(1)} %copy-done.2), kind=kOutput, calls=%fused_computation.11 | convolution fusion | flops 8413184 | bytes 1126400 | tf_op jit(solution)/shard_map/dot_general | solution.py:119
  116.7 6.7 %fusion = bf16[1536,2048]{1,0:T(8,128)(2,1)S(1)} fusion(f32[1536,2048]{1,0:T(8,128)} %bitcast_add_fusion.1, bf16[1536,128]{1,0:T(8,128)(2,1)S(1)} %all_gather.20, f32[8,2048]{1,0:T(8,128)S(1)} %convolution_add_fusion.1, bf16[384,2048]{1,0:T(8,128)(2,1)} %all-gather.8.cloned.1.call-done), kind=kOutput, calls=%fused_computation.1 | convolution fusion | flops 817889280 | bytes 19857408 | tf_op jit(solution)/shard_map/dot_general | solution.py:121
  123.4 5.4 %fusion.11 = f32[1536]{0:T(1024)S(1)} fusion(f32[512]{0:T(512)S(1)} %convert_element_type.72, bf16[1536,2048]{1,0:T(8,128)(2,1)S(1)} %fusion, s32[]{:T(128)S(6)} %select_n.127, f32[512]{0:T(512)S(1)} %bitcast.49, bf16[2,2048,512]{2,1,0:T(8,128)(2,1)S(1)} %copy-done.4, f32[1536,2048]{1,0:T(8,128)} %bitcast_add_fusion.1), kind=kOutput, calls=%fused_computation.18 | convolution fusion | flops 3226728960 | bytes 11544580 | tf_op jit(solution)/shard_map/dot_general | solution.py:127
  129.0 9.3 %psum.15 = f32[8,192]{1,0:T(8,128)} all-reduce(f32[8,192]{1,0:T(8,128)S(1)} %reshape.208), channel_id=1, replica_groups=mesh['leaf'=2,'user'=4,'tensor'=4] {'tensor'}, use_global_device_ids=true, to_apply=%region_9.10 | all-reduce | flops 1536 | bytes 12288 | tf_op jit(solution)/shard_map/psum | solution.py:135
  (46 shorter events, 1.2 us)
Async XLA Ops:
  7.2 8.3 %copy-start = (bf16[2048,128]{1,0:T(8,128)(2,1)S(1)}, bf16[2048,128]{1,0:T(8,128)(2,1)}, u32[]{:S(2)}) copy-start(bf16[2048,128]{1,0:T(8,128)(2,1)} %param.19) | copy-start | bytes 1572868
  7.2 44.3 %all-gather.6.cloned.1.call-start = ((), (), s32[]{:S(2)}) async-start(), calls=%async_computation.1 | async-start | bytes 1966080 | tf_op jit(solution)/shard_map/all_gather | solution.py:71
  16.8 77.3 %all-to-all-start = ((bf16[8,48,128]{2,1,0:T(8,128)(2,1)}), bf16[8,48,128]{2,1,0:T(8,128)(2,1)S(1)}, u32[]{:S(2)}, u32[]{:S(2)}) async-start(bf16[8,48,128]{2,1,0:T(8,128)(2,1)} %bitcast.5), calls=%async_computation | async-start | bytes 196608 | tf_op jit(solution)/shard_map/all_to_all | solution.py:110
  23.1 92.1 %all-gather.8.cloned.1.call-start = ((), (), s32[]{:S(2)}) async-start(), calls=%async_computation.2 | async-start | bytes 1966080 | tf_op jit(solution)/shard_map/all_gather | solution.py:73
  49.7 5.7 %copy-start.5 = (bf16[2048,128]{1,0:T(8,128)(2,1)S(1)}, bf16[2048,128]{1,0:T(8,128)(2,1)}, u32[]{:S(2)}) copy-start(bf16[2048,128]{1,0:T(8,128)(2,1)} %param.18) | copy-start | bytes 1572868
  49.7 6.6 %copy-start.6 = (bf16[128,1024]{1,0:T(8,128)(2,1)S(1)}, bf16[128,1024]{1,0:T(8,128)(2,1)}, u32[]{:S(2)}) copy-start(bf16[128,1024]{1,0:T(8,128)(2,1)} %param.21) | copy-start | bytes 786436
  49.7 6.6 %copy-start.7 = (f32[1024]{0:T(1024)S(1)}, f32[1024]{0:T(1024)}, u32[]{:S(2)}) copy-start(f32[1024]{0:T(1024)} %param.22) | copy-start | bytes 12292
  55.3 25.3 %copy-start.3 = (f32[2,512]{1,0:T(2,128)S(1)}, f32[2,512]{1,0:T(2,128)}, u32[]{:S(2)}) copy-start(f32[2,512]{1,0:T(2,128)} %param.26) | copy-start | bytes 12292
  55.3 53.3 %copy-start.1 = (bf16[384,2048]{1,0:T(8,128)(2,1)S(1)}, bf16[384,2048]{1,0:T(8,128)(2,1)}, u32[]{:S(2)}) copy-start(bf16[384,2048]{1,0:T(8,128)(2,1)} %all-gather.6.cloned.1.call-done) | copy-start | bytes 4718596
  55.3 53.3 %copy-start.2 = (bf16[8,128]{1,0:T(8,128)(2,1)S(1)}, bf16[8,128]{1,0:T(8,128)(2,1)}, u32[]{:S(2)}) copy-start(bf16[8,128]{1,0:T(8,128)(2,1)} %param.14) | copy-start | bytes 6148
  116.7 6.7 %copy-start.4 = (bf16[2,2048,512]{2,1,0:T(8,128)(2,1)S(1)}, bf16[2,2048,512]{2,1,0:T(8,128)(2,1)}, u32[]{:S(2)}) copy-start(bf16[2,2048,512]{2,1,0:T(8,128)(2,1)} %param.25) | copy-start | bytes 12582916
Sparse Core Ops, SparseCore 0:
  9.6 41.9 all-gather.5
  55.5 37.4 all-gather.7
where the time goes:
time: 146 us; the launch traced here: 145 us
  blocking collectives  84.2 us (58%)
  matrix products  30.7 us (21%)
  between operations  14.2 us (10%)
  starting transfers between devices  6.43 us (4%)
  other arithmetic  3.65 us (2%)
  local copies, waits for them, and re-layouts  3.47 us (2%)
  waiting for transfers between devices  2.5 us (2%)
    all_gather x1, blocking collectives, per_device(): node_ids = lax.all_gather(beam_nodes.reshape(-1), BOTH, axis=0)  21.6 us
    psum x1, blocking collectives, per_device(): lax.psum(jnp.concatenate([numerator.reshape(-1), back.reshape(-1)]), BOTH)  21.1 us
    all_gather x1, blocking collectives, per_device(): item_rows = lax.all_gather(run_rows, 'tensor', axis=0, tiled=True)  14.2 us
    all_gather x1, blocking collectives, per_device(): bias_all = lax.all_gather(cross_b[0], 'tensor', axis=0, tiled=True)  12.6 us
    psum x1, blocking collectives, per_device(): logit = lax.psum(partial, 'tensor').reshape(users, items)  9.34 us
    dot_general x1, matrix products, per_device(): jnp.dot(item_rows, first_all[two:], preferred_element_type=F32)  6.74 us
    dot_general x1, matrix products, per_device(): jnp.dot(item_rows, proj_all[two:], preferred_element_type=F32)  6.37 us
    all_to_all x1, starting transfers between devices, per_device(): lax.all_to_all(sent, BOTH, split_axis=0, concat_axis=0, tiled=True)  6.35 us
  transfers between devices with their start and end apart: 3, of which 1 were waited for; matrix products, arithmetic and copies ran while one was open for 17% of the time, Pallas kernels for 0%

commit v1 on v0

--- a/solution.py
+++ b/solution.py
@@ -71,7 +71,14 @@
     proj_all = lax.all_gather(proj_in, "tensor", axis=1, tiled=True)
     first_here = jnp.dot(proj_all, cross_w[0], preferred_element_type=F32).astype(BF16)
     first_all = lax.all_gather(first_here, "tensor", axis=1, tiled=True)
-    bias_all = lax.all_gather(cross_b[0], "tensor", axis=0, tiled=True)
+    ways = lax.axis_size("tensor")
+    pieces = [cross_b[0]]
+    for far in range(1, ways):
+        pieces.append(
+            lax.ppermute(pieces[far - 1], "tensor", [(d, (d - 1) % ways) for d in range(ways)])
+        )
+    line = jnp.concatenate(pieces, axis=0)
+    bias_all = jnp.roll(line, lax.axis_index("tensor") * cross_b[0].shape[0], axis=0)
     requests = users * beam
     cap_b = max(2, -(-requests // owners))
     node_ids = lax.all_gather(beam_nodes.reshape(-1), BOTH, axis=0)

time: 146 us -> 140 us (0.959)
  blocking collectives: 84.2 us -> 73.6 us
  starting transfers between devices: 6.43 us -> 10.9 us
  waiting for transfers between devices: 2.5 us -> 6.15 us
  matrix products: 30.7 us -> 27.2 us
    all_gather x1 -> x0, blocking collectives: 12.6 us -> none  [per_device(): bias_all = lax.all_gather(cross_b[0], 'tensor', axis=0, tiled=True)]
    ppermute x0 -> x3, starting transfers between devices: none -> 7.49 us  [per_device(): lax.ppermute(pieces[far - 1], 'tensor', [(d, (d - 1) % ways) for d in ran...]
    ppermute x0 -> x3, waiting for transfers between devices: none -> 5.43 us  [per_device(): lax.ppermute(pieces[far - 1], 'tensor', [(d, (d - 1) % ways) for d in ran...]
    dot_general x1, matrix products: 6.74 us -> 2.82 us  [per_device(): jnp.dot(item_rows, first_all[two:], preferred_element_type=F32)]
    all_to_all x1, starting transfers between devices: 6.35 us -> 3.36 us  [per_device(): lax.all_to_all(sent, BOTH, split_axis=0, concat_axis=0, tiled=True)]
    dot_general x1, matrix products: 5.43 us -> 8.26 us  [per_device(): second = jnp.dot(x1, cross_w[1], preferred_element_type=F32)]
    all_gather x1, blocking collectives: 14.2 us -> 16.7 us  [per_device(): item_rows = lax.all_gather(run_rows, 'tensor', axis=0, tiled=True)]
    all_gather x1, waiting for transfers between devices: 1.8 us -> 0.02 us  [per_device(): proj_all = lax.all_gather(proj_in, 'tensor', axis=1, tiled=True)]
  transfers between devices with their start and end apart: 3 -> 6, of which waited for: 1 -> 2; matrix products, arithmetic and copies ran while one was open for 17% -> 11% of each run, Pallas kernels for 0% -> 0%
where the time goes in v1:
time: 140 us
  blocking collectives  73.6 us (53%)
  matrix products  27.2 us (19%)
  between operations  14.3 us (10%)
  starting transfers between devices  10.9 us (8%)
  waiting for transfers between devices  6.15 us (4%)
  local copies, waits for them, and re-layouts  4.42 us (3%)
  other arithmetic  3 us (2%)
    all_gather x1, blocking collectives, per_device(): node_ids = lax.all_gather(beam_nodes.reshape(-1), BOTH, axis=0)  21.6 us
    psum x1, blocking collectives, per_device(): lax.psum(jnp.concatenate([numerator.reshape(-1), back.reshape(-1)]), BOTH)  20.1 us
    all_gather x1, blocking collectives, per_device(): item_rows = lax.all_gather(run_rows, 'tensor', axis=0, tiled=True)  16.7 us
    psum x1, blocking collectives, per_device(): logit = lax.psum(partial, 'tensor').reshape(users, items)  10.8 us
    dot_general x1, matrix products, per_device(): second = jnp.dot(x1, cross_w[1], preferred_element_type=F32)  8.26 us
    ppermute x3, starting transfers between devices, per_device(): lax.ppermute(pieces[far - 1], 'tensor', [(d, (d - 1) % ways) for d in ran...  7.49 us
    dot_general x1, matrix products, per_device(): jnp.dot(item_rows, proj_all[two:], preferred_element_type=F32)  5.96 us
    ppermute x3, waiting for transfers between devices, per_device(): lax.ppermute(pieces[far - 1], 'tensor', [(d, (d - 1) % ways) for d in ran...  5.43 us
  transfers between devices with their start and end apart: 6, of which 2 were waited for; matrix products, arithmetic and copies ran while one was open for 11% of the time, Pallas kernels for 0%

profile of v1, /device:TPU:0, one launch (start us, length us, event | category | flops | bytes accessed | tf_op | source)
XLA Modules:
  0.0 139.6 jit_solution(3621479188436394729)
XLA Ops:
  7.3 0.7 all-gather.5.cloned.1.call-update
  8.0 0.8 fusion.69
  8.7 5.1 %collective-permute-start = (f32[512]{0:T(512)S(1)}, f32[512]{0:T(512)S(1)}, u32[]{:S(2)}, u32[]{:S(2)}) collective-permute-start(f32[512]{0:T(512)S(1)} %bitcast.47), channel_id=1, source_target_pairs={{0,3},{1,0},{2,1},{3,2},{4,7},{5,4},{6,5},{7,6},{8,11},{9,8},{10,9... | collective-permute-start | bytes 6152 | tf_op jit(solution)/shard_map/ppermute | solution.py:78
  13.8 0.8 reshape.211
  14.6 4.4 %all-gather.1 = s32[2,1,1536]{2,1,0:T(1,128)S(1)} all-gather(s32[1,1,1536]{2,1,0:T(1,128)S(1)} %reshape.211), channel_id=1, replica_groups=mesh['leaf'=2,'user'=4,'tensor'=4] {'leaf'}, dimensions={0}, use_global_device_ids=true | all-gather | bytes 18432 | tf_op jit(solution)/shard_map/all_gather | solution.py:113
  19.0 0.8 select_reduce_fusion.1
  20.4 1.3 fusion.18
  21.7 3.4 %all-to-all-start = ((bf16[8,48,128]{2,1,0:T(8,128)(2,1)}), bf16[8,48,128]{2,1,0:T(8,128)(2,1)S(1)}, u32[]{:S(2)}, u32[]{:S(2)}) async-start(bf16[8,48,128]{2,1,0:T(8,128)(2,1)} %bitcast.5), calls=%async_computation | async-start | bytes 196608 | tf_op jit(solution)/shard_map/all_to_all | solution.py:117
  25.1 0.8 reshape.209
  25.9 21.6 %all-gather = s32[8,1,128]{2,1,0:T(1,128)S(1)} all-gather(s32[1,1,128]{2,1,0:T(1,128)S(1)} %reshape.209), channel_id=1, replica_groups=mesh['leaf'=2,'user'=4,'tensor'=4] {'leaf','tensor'}, dimensions={0}, use_global_device_ids=true | all-gather | bytes 4608 | tf_op jit(solution)/shard_map/all_gather | solution.py:84
  47.5 0.7 select_reduce_fusion.2
  48.4 0.3 select_reduce_fusion.4
  49.0 0.7 reshape.216
  49.7 1.4 %convolution_convert_fusion.1 = bf16[128,128]{1,0:T(8,128)(2,1)S(1)} fusion(bf16[2048,128]{1,0:T(8,128)(2,1)} %param.18, s32[128]{0:T(128)S(1)} %sub.46), kind=kOutput, calls=%fused_computation.23 | convolution fusion | flops 67387392 | bytes 557568 | tf_op jit(solution)/shard_map/dot_general | solution.py:34
  51.1 0.4 fusion.19
  51.5 0.4 add_divide_fusion
  52.1 3.9 %fusion.14 = bf16[384,512]{1,0:T(8,128)(2,1)} fusion(bf16[384,2048]{1,0:T(8,128)(2,1)} %all-gather.5.cloned.1.call-done, bf16[2,2048,512]{2,1,0:T(8,128)(2,1)} %param.25), kind=kOutput, calls=%fused_computation.18 | convolution fusion | flops 805502976 | bytes 4063232 | tf_op jit(solution)/shard_map/dot_general | solution.py:72
  56.1 0.3 convolution_bitcast_fusion
  56.4 20.1 %psum.14 = f32[2048]{0:T(1024)S(1)} all-reduce(f32[2048]{0:T(1024)S(1)} %pad_maximum_fusion), channel_id=1, replica_groups=mesh['leaf'=2,'user'=4,'tensor'=4] {'leaf','tensor'}, use_global_device_ids=true, to_apply=%region_4.5 | all-reduce | flops 2048 | bytes 16384 | tf_op jit(solution)/shard_map/psum | solution.py:105
  76.8 0.6 fusion.67
  77.5 0.7 reshape.204
  78.1 0.3 collective-permute-start.1
  78.5 3.6 %collective-permute-done.1 = f32[512]{0:T(512)S(1)} collective-permute-done((f32[512]{0:T(512)S(1)}, f32[512]{0:T(512)S(1)}, u32[]{:S(2)}, u32[]{:S(2)}) %collective-permute-start.1) | collective-permute-done | bytes 2080 | tf_op jit(solution)/shard_map/ppermute | solution.py:78
  82.1 2.1 %collective-permute-start.2 = (f32[512]{0:T(512)S(1)}, f32[512]{0:T(512)S(1)}, u32[]{:S(2)}, u32[]{:S(2)}) collective-permute-start(f32[512]{0:T(512)S(1)} %collective-permute-done.1), channel_id=1, source_target_pairs={{0,3},{1,0},{2,1},{3,2},{4,7},{5,4},{6,5},{7,6},{8,11},{9,8},{10,9... | collective-permute-start | bytes 6152 | tf_op jit(solution)/shard_map/ppermute | solution.py:78
  84.1 1.8 %collective-permute-done.2 = f32[512]{0:T(512)S(1)} collective-permute-done((f32[512]{0:T(512)S(1)}, f32[512]{0:T(512)S(1)}, u32[]{:S(2)}, u32[]{:S(2)}) %collective-permute-start.2) | collective-permute-done | bytes 2080 | tf_op jit(solution)/shard_map/ppermute | solution.py:78
  86.1 0.3 convolution_convert_fusion
  86.4 16.7 %all_gather.17 = bf16[1536,128]{1,0:T(8,128)(2,1)S(1)} all-gather(bf16[384,128]{1,0:T(8,128)(2,1)S(1)} %convolution_convert_fusion), channel_id=1, replica_groups=mesh['leaf'=2,'user'=4,'tensor'=4] {'tensor'}, dimensions={0}, use_global_device_ids=true | all-gather | bytes 491520 | tf_op jit(solution)/shard_map/all_gather | solution.py:122
  103.3 1.5 %broadcast_add_fusion = f32[8,2048]{1,0:T(8,128)S(1)} fusion(f32[2048]{0:T(1024)S(1)} %dynamic_slice.19, bf16[384,2048]{1,0:T(8,128)(2,1)} %all-gather.7.cloned.1.call-done, bf16[8,128]{1,0:T(8,128)(2,1)S(1)} %get-tuple-element.5, bf16[8,128]{1,0:T(8,128)(2,1)S(1)} %copy-done.3), kind=kOutput, calls=%fused_computation.64 | convolution fusion | flops 8413184 | bytes 1126400 | tf_op jit(solution)/shard_map/dot_general | solution.py:126
  104.8 2.8 %fusion.27 = f32[1536,2048]{1,0:T(8,128)S(1)} fusion(bf16[1536,128]{1,0:T(8,128)(2,1)S(1)} %all_gather.17, bf16[384,2048]{1,0:T(8,128)(2,1)} %all-gather.7.cloned.1.call-done), kind=kOutput, calls=%fused_computation.43 | convolution fusion | flops 805306368 | bytes 13500416 | tf_op jit(solution)/shard_map/dot_general | solution.py:128
  107.7 6.0 %fusion = (bf16[1536,2048]{1,0:T(8,128)(2,1)}, bf16[1536,2048]{1,0:T(8,128)(2,1)}) fusion(f32[1536,2048]{1,0:T(8,128)S(1)} %fusion.27, f32[8,2048]{1,0:T(8,128)S(1)} %broadcast_add_fusion, f32[8,2048]{1,0:T(8,128)S(1)} %fusion.24, bf16[1536,128]{1,0:T(8,128)(2,1)S(1)} %all_gather.17, bf16[384,2048]{1,0:T(8,128)(2,1)S(1)} %copy-done.1), kind=kOutput, calls=%fused_computation.1 | convolution fusion | flops 824180736 | bytes 26214400 | tf_op jit(solution)/shard_map/dot_general | solution.py:127
  113.6 8.3 %fusion.11 = f32[1536]{0:T(1024)S(1)} fusion(f32[512]{0:T(512)S(1)} %convert_element_type.72, bf16[1536,2048]{1,0:T(8,128)(2,1)} %get-tuple-element.13, s32[]{:T(128)S(6)} %select_n.139, f32[512]{0:T(512)S(1)} %bitcast.51, bf16[2,2048,512]{2,1,0:T(8,128)(2,1)} %param.25, bf16[1536,2048]{1,0:T(8,128)(2,1)} %get-tuple-element.14), kind=kOutput, calls=%fused_computation.17 | convolution fusion | flops 3226728960 | bytes 11544580 | tf_op jit(solution)/shard_map/dot_general | solution.py:134
  122.0 10.8 %psum.15 = f32[8,192]{1,0:T(8,128)} all-reduce(f32[8,192]{1,0:T(8,128)S(1)} %reshape.208), channel_id=1, replica_groups=mesh['leaf'=2,'user'=4,'tensor'=4] {'tensor'}, use_global_device_ids=true, to_apply=%region_9.10 | all-reduce | flops 1536 | bytes 12288 | tf_op jit(solution)/shard_map/psum | solution.py:142
  (59 shorter events, 2.1 us)
Async XLA Ops:
  7.2 13.2 %copy-start = (bf16[2048,128]{1,0:T(8,128)(2,1)S(1)}, bf16[2048,128]{1,0:T(8,128)(2,1)}, u32[]{:S(2)}) copy-start(bf16[2048,128]{1,0:T(8,128)(2,1)} %param.19) | copy-start | bytes 1572868
  7.2 43.9 %copy-start.3 = (bf16[8,128]{1,0:T(8,128)(2,1)S(1)}, bf16[8,128]{1,0:T(8,128)(2,1)}, u32[]{:S(2)}) copy-start(bf16[8,128]{1,0:T(8,128)(2,1)} %param.14) | copy-start | bytes 6148
  7.2 43.9 %copy-start.2 = (bf16[128,1024]{1,0:T(8,128)(2,1)S(1)}, bf16[128,1024]{1,0:T(8,128)(2,1)}, u32[]{:S(2)}) copy-start(bf16[128,1024]{1,0:T(8,128)(2,1)} %param.20) | copy-start | bytes 786436
  7.2 44.3 %copy-start.6 = (f32[1024]{0:T(1024)S(1)}, f32[1024]{0:T(1024)}, u32[]{:S(2)}) copy-start(f32[1024]{0:T(1024)} %param.22) | copy-start | bytes 12292
  7.2 44.3 %copy-start.5 = (bf16[128,1024]{1,0:T(8,128)(2,1)S(1)}, bf16[128,1024]{1,0:T(8,128)(2,1)}, u32[]{:S(2)}) copy-start(bf16[128,1024]{1,0:T(8,128)(2,1)} %param.21) | copy-start | bytes 786436
  7.2 44.8 %all-gather.5.cloned.1.call-start = ((), (), s32[]{:S(2)}) async-start(), calls=%async_computation.1 | async-start | bytes 1966080 | tf_op jit(solution)/shard_map/all_gather | solution.py:71
  8.7 69.4 %collective-permute-start = (f32[512]{0:T(512)S(1)}, f32[512]{0:T(512)S(1)}, u32[]{:S(2)}, u32[]{:S(2)}) collective-permute-start(f32[512]{0:T(512)S(1)} %bitcast.47), channel_id=1, source_target_pairs={{0,3},{1,0},{2,1},{3,2},{4,7},{5,4},{6,5},{7,6},{8,11},{9,8},{10,9... | collective-permute-start | bytes 6152 | tf_op jit(solution)/shard_map/ppermute | solution.py:78
  21.7 64.4 %all-to-all-start = ((bf16[8,48,128]{2,1,0:T(8,128)(2,1)}), bf16[8,48,128]{2,1,0:T(8,128)(2,1)S(1)}, u32[]{:S(2)}, u32[]{:S(2)}) async-start(bf16[8,48,128]{2,1,0:T(8,128)(2,1)} %bitcast.5), calls=%async_computation | async-start | bytes 196608 | tf_op jit(solution)/shard_map/all_to_all | solution.py:117
  25.1 78.3 %all-gather.7.cloned.1.call-start = ((), (), s32[]{:S(2)}) async-start(), calls=%async_computation.2 | async-start | bytes 1966080 | tf_op jit(solution)/shard_map/all_gather | solution.py:73
  52.0 25.4 %copy-start.4 = (bf16[512]{0:T(512)(128)(2,1)S(1)}, bf16[512]{0:T(512)(128)(2,1)}, u32[]{:S(2)}) copy-start(bf16[512]{0:T(512)(128)(2,1)} %param.27) | copy-start | bytes 3076
  52.1 51.0 %copy-start.1 = (bf16[384,2048]{1,0:T(8,128)(2,1)S(1)}, bf16[384,2048]{1,0:T(8,128)(2,1)}, u32[]{:S(2)}) copy-start(bf16[384,2048]{1,0:T(8,128)(2,1)} %all-gather.5.cloned.1.call-done) | copy-start | bytes 4718596
  78.1 3.9 %collective-permute-start.1 = (f32[512]{0:T(512)S(1)}, f32[512]{0:T(512)S(1)}, u32[]{:S(2)}, u32[]{:S(2)}) collective-permute-start(f32[512]{0:T(512)S(1)} %collective-permute-done), channel_id=1, source_target_pairs={{0,3},{1,0},{2,1},{3,2},{4,7},{5,4},{6,5},{7,6},{8,11},{9,8},{10,9... | collective-permute-start | bytes 6152 | tf_op jit(solution)/shard_map/ppermute | solution.py:78
  82.1 3.9 %collective-permute-start.2 = (f32[512]{0:T(512)S(1)}, f32[512]{0:T(512)S(1)}, u32[]{:S(2)}, u32[]{:S(2)}) collective-permute-start(f32[512]{0:T(512)S(1)} %collective-permute-done.1), channel_id=1, source_target_pairs={{0,3},{1,0},{2,1},{3,2},{4,7},{5,4},{6,5},{7,6},{8,11},{9,8},{10,9... | collective-permute-start | bytes 6152 | tf_op jit(solution)/shard_map/ppermute | solution.py:78
Sparse Core Ops, SparseCore 0:
  9.6 41.9 all-gather.4
  56.1 39.4 all-gather.6
